TPU v7x, 128 devices: a whole 4x4x4 slice. The times are simulated.
128 devices in a mesh: occ: 8 (over y_hi, z), virt: 16 (over x, y_lo, core).
Axes of the slice: x: 4, y: 4 (y_hi: 2, y_lo: 2; y = y_hi * 2 + y_lo), z: 4, core: 2. Of those that a mesh axis runs over, the one named last changes fastest.
Arguments:
- basis_integrals: bfloat16 [32, 1280, 2048], P(None, 'virt', 'occ'), may hold values from -2 to 2
- group_sizes: int32 [8], replicated, may hold values from 1 to 6, 32 in all
- orbital_order: int32 [32], replicated, may hold values from 0 to 31, each once
- eps_occ: float32 [32], replicated, may hold values from -1.5 to -0.3
- eps_vir: float32 [1280], replicated, may hold values from 0.2 to 2.5
Outputs:
- density: bfloat16 [8, 6, 1280, 2048], P('occ', None, 'virt')
Inputs may be any that keep to these rules, and one draw needn't show every extreme that they name: `group_sizes`: each group holds 1 to 6 orbitals, 32 together, and some group holds exactly 6. `orbital_order`: each window orbital appears once.
All inputs are finite; a program needn't handle non-finite values.
Results may differ from a plain program's by a relative error of at most 0.0034.
Values may be sent and summed in bfloat16 or wider, within the bound.
A program may use at most 64 MiB of HBM per device.

v0:
```python
import jax
import jax.numpy as jnp
from jax import lax
from jax.sharding import PartitionSpec as P

CAP = 6


def shifted(x, axis, by):
    length = lax.axis_size(axis)
    return lax.ppermute(x, axis, [(i, (i + by) % length) for i in range(length)])


def advance(passing):
    return shifted(passing, "virt", 1)


def on_device(basis_integrals, group_sizes, orbital_order, eps_occ, eps_vir):
    n_virt = lax.axis_size("virt")
    me_occ = lax.axis_index("occ")
    me_virt = lax.axis_index("virt")
    vir_width = basis_integrals.shape[1]
    window = basis_integrals.shape[0]
    slot_index = jnp.arange(CAP, dtype=jnp.int32)
    offsets = jnp.cumsum(group_sizes) - group_sizes
    occupied = slot_index[None, :] < group_sizes[:, None]
    position = jnp.clip(offsets[:, None] + slot_index[None, :], 0, window - 1)
    orbital = jnp.where(occupied, orbital_order[position], 0)
    slot_mask = jnp.where(occupied, 1.0, 0.0).astype(jnp.bfloat16)
    outgoing = basis_integrals[orbital] * slot_mask[:, :, None, None]
    arrived = lax.all_to_all(outgoing, "occ", split_axis=0, concat_axis=3, tiled=True)
    resident = arrived.reshape(CAP * vir_width, arrived.shape[3])
    my_orbitals = lax.dynamic_index_in_dim(orbital, me_occ, 0, keepdims=False)
    my_alive = lax.dynamic_index_in_dim(occupied, me_occ, 0, keepdims=False)
    occ_energy = jnp.where(my_alive, eps_occ[my_orbitals], jnp.float32(0.0))
    own_energy = lax.dynamic_slice_in_dim(eps_vir, me_virt * vir_width, vir_width)
    row_gap = (occ_energy[:, None] - own_energy[None, :]).reshape(-1)

    def contribute(running, passing, anchor):
        vir_energy = lax.dynamic_slice_in_dim(eps_vir, anchor * vir_width, vir_width)
        col_gap = (occ_energy[:, None] - vir_energy[None, :]).reshape(-1)
        coulomb = lax.dot_general(
            resident, passing, (((1,), (1,)), ((), ())), preferred_element_type=jnp.float32
        )
        amplitude = coulomb / (row_gap[:, None] + col_gap[None, :])
        amp_four = amplitude.reshape(CAP, vir_width, CAP, vir_width)
        combined = (2.0 * amp_four - amp_four.transpose(2, 1, 0, 3)).reshape(
            CAP * vir_width, CAP * vir_width
        )
        combined = combined.astype(jnp.bfloat16)
        return running + jnp.dot(combined, passing, preferred_element_type=jnp.float32)

    running = contribute(jnp.zeros(resident.shape, jnp.float32), resident, me_virt)

    def turn(turn_index, loop_state):
        running, passing = loop_state
        passing = advance(passing)
        running = contribute(running, passing, jnp.mod(me_virt - turn_index, n_virt))
        return (running, passing)

    running, passing = lax.fori_loop(1, n_virt, turn, (running, resident))
    return running.reshape(1, CAP, vir_width, running.shape[1]).astype(jnp.bfloat16)


def solution(mesh):
    return jax.shard_map(
        on_device,
        mesh=mesh,
        in_specs=(P(None, "virt", "occ"), P(), P(), P(), P()),
        out_specs=P("occ", None, "virt", None),
        check_vma=False,
    )
```

profile of v0, /device:TPU:0, one launch (start us, length us, event | category | flops | bytes accessed | tf_op | source)
XLA Modules:
  0.0 726.4 jit_solution(12116262121798427821)
XLA Ops:
  5.7 8.2 %all-to-all-start = ((bf16[8,6,80,256]{3,2,1,0:T(8,128)(2,1)}), bf16[8,6,80,256]{3,2,1,0:T(8,128)(2,1)S(1)}, u32[]{:S(2)}, u32[]{:S(2)}) async-start(bf16[8,6,80,256]{3,2,1,0:T(8,128)(2,1)} %broadcast_multiply_fusion), calls=%async_computation | async-start | bytes 3932160 | tf_op jit(solution)/shard_map/all_to_all | solution.py:31
  15.8 23.2 %all-to-all-done = bf16[8,6,80,256]{3,2,1,0:T(8,128)(2,1)S(1)} async-done(((bf16[8,6,80,256]{3,2,1,0:T(8,128)(2,1)}), bf16[8,6,80,256]{3,2,1,0:T(8,128)(2,1)S(1)}, u32[]{:S(2)}, u32[]{:S(2)}) %all-to-all-start) | async-done | bytes 1966112 | tf_op jit(solution)/shard_map/all_to_all | solution.py:31
  41.9 3.1 copy.49
  45.0 4.3 convolution_divide_fusion.1
  52.3 4.6 fusion.6
  56.9 665.8 %while.19 = (s32[]{:T(128)}, f32[480,2048]{1,0:T(8,128)}, bf16[480,2048]{1,0:T(8,128)(2,1)}, bf16[480,2048]{1,0:T(8,128)(2,1)}, f32[6]{0:T(128)S(1)}, /*index=5*...) while((s32[]{:T(128)}, f32[480,2048]{1,0:T(8,128)}, ...), condition=%wide.region_2.3_spmd.clone.clone, body=%wide.region_1.2_spmd.clone.clone.sunk | while | flops 1889572864 | bytes 79213272 | solution.py:61
  57.9 25.4 %collective-permute-done = bf16[480,2048]{1,0:T(8,128)(2,1)S(1)} collective-permute-done((bf16[480,2048]{1,0:T(8,128)(2,1)}, bf16[480,2048]{1,0:T(8,128)(2,1)S(1)}, u32[]{:S(2)}, u32[]{:S(2)}) %collective-permute-start) | collective-permute-done | bytes 1966112 | tf_op jit(solution)/shard_map/while/body/eval_jaxpr/ppermute | solution.py:11
  84.6 3.7 convolution_divide_fusion.3
  91.7 2.4 convert_element_type.55
  97.0 2.5 convolution_add_fusion.2
  102.3 25.4 %collective-permute-done = bf16[480,2048]{1,0:T(8,128)(2,1)S(1)} collective-permute-done((bf16[480,2048]{1,0:T(8,128)(2,1)}, bf16[480,2048]{1,0:T(8,128)(2,1)S(1)}, u32[]{:S(2)}, u32[]{:S(2)}) %collective-permute-start) | collective-permute-done | bytes 1966112 | tf_op jit(solution)/shard_map/while/body/eval_jaxpr/ppermute | solution.py:11
  129.0 3.7 convolution_divide_fusion.3
  136.1 2.4 convert_element_type.55
  141.4 2.5 convolution_add_fusion.2
  146.7 25.4 %collective-permute-done = bf16[480,2048]{1,0:T(8,128)(2,1)S(1)} collective-permute-done((bf16[480,2048]{1,0:T(8,128)(2,1)}, bf16[480,2048]{1,0:T(8,128)(2,1)S(1)}, u32[]{:S(2)}, u32[]{:S(2)}) %collective-permute-start) | collective-permute-done | bytes 1966112 | tf_op jit(solution)/shard_map/while/body/eval_jaxpr/ppermute | solution.py:11
  173.4 3.7 convolution_divide_fusion.3
  180.5 2.4 convert_element_type.55
  185.7 2.5 convolution_add_fusion.2
  191.1 25.4 %collective-permute-done = bf16[480,2048]{1,0:T(8,128)(2,1)S(1)} collective-permute-done((bf16[480,2048]{1,0:T(8,128)(2,1)}, bf16[480,2048]{1,0:T(8,128)(2,1)S(1)}, u32[]{:S(2)}, u32[]{:S(2)}) %collective-permute-start) | collective-permute-done | bytes 1966112 | tf_op jit(solution)/shard_map/while/body/eval_jaxpr/ppermute | solution.py:11
  217.8 3.7 convolution_divide_fusion.3
  224.9 2.4 convert_element_type.55
  230.1 2.5 convolution_add_fusion.2
  235.5 25.4 %collective-permute-done = bf16[480,2048]{1,0:T(8,128)(2,1)S(1)} collective-permute-done((bf16[480,2048]{1,0:T(8,128)(2,1)}, bf16[480,2048]{1,0:T(8,128)(2,1)S(1)}, u32[]{:S(2)}, u32[]{:S(2)}) %collective-permute-start) | collective-permute-done | bytes 1966112 | tf_op jit(solution)/shard_map/while/body/eval_jaxpr/ppermute | solution.py:11
  262.1 3.7 convolution_divide_fusion.3
  269.2 2.4 convert_element_type.55
  274.5 2.5 convolution_add_fusion.2
  279.9 25.4 %collective-permute-done = bf16[480,2048]{1,0:T(8,128)(2,1)S(1)} collective-permute-done((bf16[480,2048]{1,0:T(8,128)(2,1)}, bf16[480,2048]{1,0:T(8,128)(2,1)S(1)}, u32[]{:S(2)}, u32[]{:S(2)}) %collective-permute-start) | collective-permute-done | bytes 1966112 | tf_op jit(solution)/shard_map/while/body/eval_jaxpr/ppermute | solution.py:11
  306.5 3.7 convolution_divide_fusion.3
  313.6 2.4 convert_element_type.55
  318.9 2.5 convolution_add_fusion.2
  324.2 25.4 %collective-permute-done = bf16[480,2048]{1,0:T(8,128)(2,1)S(1)} collective-permute-done((bf16[480,2048]{1,0:T(8,128)(2,1)}, bf16[480,2048]{1,0:T(8,128)(2,1)S(1)}, u32[]{:S(2)}, u32[]{:S(2)}) %collective-permute-start) | collective-permute-done | bytes 1966112 | tf_op jit(solution)/shard_map/while/body/eval_jaxpr/ppermute | solution.py:11
  350.9 3.7 convolution_divide_fusion.3
  358.0 2.4 convert_element_type.55
  363.3 2.5 convolution_add_fusion.2
  368.6 25.4 %collective-permute-done = bf16[480,2048]{1,0:T(8,128)(2,1)S(1)} collective-permute-done((bf16[480,2048]{1,0:T(8,128)(2,1)}, bf16[480,2048]{1,0:T(8,128)(2,1)S(1)}, u32[]{:S(2)}, u32[]{:S(2)}) %collective-permute-start) | collective-permute-done | bytes 1966112 | tf_op jit(solution)/shard_map/while/body/eval_jaxpr/ppermute | solution.py:11
  395.3 3.7 convolution_divide_fusion.3
  402.4 2.4 convert_element_type.55
  407.7 2.5 convolution_add_fusion.2
  413.0 25.4 %collective-permute-done = bf16[480,2048]{1,0:T(8,128)(2,1)S(1)} collective-permute-done((bf16[480,2048]{1,0:T(8,128)(2,1)}, bf16[480,2048]{1,0:T(8,128)(2,1)S(1)}, u32[]{:S(2)}, u32[]{:S(2)}) %collective-permute-start) | collective-permute-done | bytes 1966112 | tf_op jit(solution)/shard_map/while/body/eval_jaxpr/ppermute | solution.py:11
  439.7 3.7 convolution_divide_fusion.3
  452.1 2.5 convolution_add_fusion.2
  457.4 25.4 %collective-permute-done = bf16[480,2048]{1,0:T(8,128)(2,1)S(1)} collective-permute-done((bf16[480,2048]{1,0:T(8,128)(2,1)}, bf16[480,2048]{1,0:T(8,128)(2,1)S(1)}, u32[]{:S(2)}, u32[]{:S(2)}) %collective-permute-start) | collective-permute-done | bytes 1966112 | tf_op jit(solution)/shard_map/while/body/eval_jaxpr/ppermute | solution.py:11
  484.1 3.7 convolution_divide_fusion.3
  491.2 2.4 convert_element_type.55
  496.5 2.5 convolution_add_fusion.2
  501.8 25.4 %collective-permute-done = bf16[480,2048]{1,0:T(8,128)(2,1)S(1)} collective-permute-done((bf16[480,2048]{1,0:T(8,128)(2,1)}, bf16[480,2048]{1,0:T(8,128)(2,1)S(1)}, u32[]{:S(2)}, u32[]{:S(2)}) %collective-permute-start) | collective-permute-done | bytes 1966112 | tf_op jit(solution)/shard_map/while/body/eval_jaxpr/ppermute | solution.py:11
  528.5 3.7 convolution_divide_fusion.3
  535.6 2.4 convert_element_type.55
  540.8 2.5 convolution_add_fusion.2
  546.2 25.4 %collective-permute-done = bf16[480,2048]{1,0:T(8,128)(2,1)S(1)} collective-permute-done((bf16[480,2048]{1,0:T(8,128)(2,1)}, bf16[480,2048]{1,0:T(8,128)(2,1)S(1)}, u32[]{:S(2)}, u32[]{:S(2)}) %collective-permute-start) | collective-permute-done | bytes 1966112 | tf_op jit(solution)/shard_map/while/body/eval_jaxpr/ppermute | solution.py:11
  572.9 3.7 convolution_divide_fusion.3
  580.0 2.4 convert_element_type.55
  585.2 2.5 convolution_add_fusion.2
  590.6 25.4 %collective-permute-done = bf16[480,2048]{1,0:T(8,128)(2,1)S(1)} collective-permute-done((bf16[480,2048]{1,0:T(8,128)(2,1)}, bf16[480,2048]{1,0:T(8,128)(2,1)S(1)}, u32[]{:S(2)}, u32[]{:S(2)}) %collective-permute-start) | collective-permute-done | bytes 1966112 | tf_op jit(solution)/shard_map/while/body/eval_jaxpr/ppermute | solution.py:11
  617.2 3.7 convolution_divide_fusion.3
  624.3 2.4 convert_element_type.55
  629.6 2.5 convolution_add_fusion.2
  635.0 25.4 %collective-permute-done = bf16[480,2048]{1,0:T(8,128)(2,1)S(1)} collective-permute-done((bf16[480,2048]{1,0:T(8,128)(2,1)}, bf16[480,2048]{1,0:T(8,128)(2,1)S(1)}, u32[]{:S(2)}, u32[]{:S(2)}) %collective-permute-start) | collective-permute-done | bytes 1966112 | tf_op jit(solution)/shard_map/while/body/eval_jaxpr/ppermute | solution.py:11
  661.6 3.7 convolution_divide_fusion.3
  674.0 2.5 convolution_add_fusion.2
  679.3 25.4 %collective-permute-done = bf16[480,2048]{1,0:T(8,128)(2,1)S(1)} collective-permute-done((bf16[480,2048]{1,0:T(8,128)(2,1)}, bf16[480,2048]{1,0:T(8,128)(2,1)S(1)}, u32[]{:S(2)}, u32[]{:S(2)}) %collective-permute-start) | collective-permute-done | bytes 1966112 | tf_op jit(solution)/shard_map/while/body/eval_jaxpr/ppermute | solution.py:11
  706.0 3.7 convolution_divide_fusion.3
  718.4 2.5 convolution_add_fusion.2
  722.7 3.7 convert_element_type.43
  (295 shorter events, 176.0 us)
Async XLA Ops:
  0.0 3.6 copy-start
  0.0 2.5 copy-start.1
  5.7 8.4 %copy-start.2 = (f32[32]{0:T(128)S(1)}, f32[32]{0:T(128)}, u32[]{:S(2)}) copy-start(f32[32]{0:T(128)} %param.10) | copy-start | bytes 388
  5.7 33.2 %all-to-all-start = ((bf16[8,6,80,256]{3,2,1,0:T(8,128)(2,1)}), bf16[8,6,80,256]{3,2,1,0:T(8,128)(2,1)S(1)}, u32[]{:S(2)}, u32[]{:S(2)}) async-start(bf16[8,6,80,256]{3,2,1,0:T(8,128)(2,1)} %broadcast_multiply_fusion), calls=%async_computation | async-start | bytes 3932160 | tf_op jit(solution)/shard_map/all_to_all | solution.py:31
  56.9 26.4 %collective-permute-start = (bf16[480,2048]{1,0:T(8,128)(2,1)}, bf16[480,2048]{1,0:T(8,128)(2,1)S(1)}, u32[]{:S(2)}, u32[]{:S(2)}) collective-permute-start(bf16[480,2048]{1,0:T(8,128)(2,1)} %get-tuple-element.334), channel_id=1, source_target_pairs={{0,1},{1,2},{2,3},{3,4},{4,5},{5,6},{6,7},{7,8},{8,9},{9,10},{10,1... | collective-permute-start | bytes 5898248 | tf_op jit(solution)/shard_map/while/body/eval_jaxpr/ppermute | solution.py:11
  90.5 3.7 copy-start.6
  94.1 2.8 copy-start.3
  99.4 1.9 copy-start.4
  101.3 26.4 %collective-permute-start = (bf16[480,2048]{1,0:T(8,128)(2,1)}, bf16[480,2048]{1,0:T(8,128)(2,1)S(1)}, u32[]{:S(2)}, u32[]{:S(2)}) collective-permute-start(bf16[480,2048]{1,0:T(8,128)(2,1)} %get-tuple-element.334), channel_id=1, source_target_pairs={{0,1},{1,2},{2,3},{3,4},{4,5},{5,6},{6,7},{7,8},{8,9},{9,10},{10,1... | collective-permute-start | bytes 5898248 | tf_op jit(solution)/shard_map/while/body/eval_jaxpr/ppermute | solution.py:11
  134.9 3.7 copy-start.6
  138.5 2.8 copy-start.3
  143.8 1.9 copy-start.4
  145.7 26.4 %collective-permute-start = (bf16[480,2048]{1,0:T(8,128)(2,1)}, bf16[480,2048]{1,0:T(8,128)(2,1)S(1)}, u32[]{:S(2)}, u32[]{:S(2)}) collective-permute-start(bf16[480,2048]{1,0:T(8,128)(2,1)} %get-tuple-element.334), channel_id=1, source_target_pairs={{0,1},{1,2},{2,3},{3,4},{4,5},{5,6},{6,7},{7,8},{8,9},{9,10},{10,1... | collective-permute-start | bytes 5898248 | tf_op jit(solution)/shard_map/while/body/eval_jaxpr/ppermute | solution.py:11
  179.3 3.7 copy-start.6
  182.9 2.8 copy-start.3
  188.2 1.9 copy-start.4
  190.1 26.4 %collective-permute-start = (bf16[480,2048]{1,0:T(8,128)(2,1)}, bf16[480,2048]{1,0:T(8,128)(2,1)S(1)}, u32[]{:S(2)}, u32[]{:S(2)}) collective-permute-start(bf16[480,2048]{1,0:T(8,128)(2,1)} %get-tuple-element.334), channel_id=1, source_target_pairs={{0,1},{1,2},{2,3},{3,4},{4,5},{5,6},{6,7},{7,8},{8,9},{9,10},{10,1... | collective-permute-start | bytes 5898248 | tf_op jit(solution)/shard_map/while/body/eval_jaxpr/ppermute | solution.py:11
  223.6 3.7 copy-start.6
  227.3 2.8 copy-start.3
  232.6 1.9 copy-start.4
  234.5 26.4 %collective-permute-start = (bf16[480,2048]{1,0:T(8,128)(2,1)}, bf16[480,2048]{1,0:T(8,128)(2,1)S(1)}, u32[]{:S(2)}, u32[]{:S(2)}) collective-permute-start(bf16[480,2048]{1,0:T(8,128)(2,1)} %get-tuple-element.334), channel_id=1, source_target_pairs={{0,1},{1,2},{2,3},{3,4},{4,5},{5,6},{6,7},{7,8},{8,9},{9,10},{10,1... | collective-permute-start | bytes 5898248 | tf_op jit(solution)/shard_map/while/body/eval_jaxpr/ppermute | solution.py:11
  268.0 3.7 copy-start.6
  271.7 2.8 copy-start.3
  277.0 1.9 copy-start.4
  278.8 26.4 %collective-permute-start = (bf16[480,2048]{1,0:T(8,128)(2,1)}, bf16[480,2048]{1,0:T(8,128)(2,1)S(1)}, u32[]{:S(2)}, u32[]{:S(2)}) collective-permute-start(bf16[480,2048]{1,0:T(8,128)(2,1)} %get-tuple-element.334), channel_id=1, source_target_pairs={{0,1},{1,2},{2,3},{3,4},{4,5},{5,6},{6,7},{7,8},{8,9},{9,10},{10,1... | collective-permute-start | bytes 5898248 | tf_op jit(solution)/shard_map/while/body/eval_jaxpr/ppermute | solution.py:11
  312.4 3.7 copy-start.6
  316.1 2.8 copy-start.3
  321.4 1.9 copy-start.4
  323.2 26.4 %collective-permute-start = (bf16[480,2048]{1,0:T(8,128)(2,1)}, bf16[480,2048]{1,0:T(8,128)(2,1)S(1)}, u32[]{:S(2)}, u32[]{:S(2)}) collective-permute-start(bf16[480,2048]{1,0:T(8,128)(2,1)} %get-tuple-element.334), channel_id=1, source_target_pairs={{0,1},{1,2},{2,3},{3,4},{4,5},{5,6},{6,7},{7,8},{8,9},{9,10},{10,1... | collective-permute-start | bytes 5898248 | tf_op jit(solution)/shard_map/while/body/eval_jaxpr/ppermute | solution.py:11
  356.8 3.7 copy-start.6
  360.5 2.8 copy-start.3
  365.8 1.9 copy-start.4
  367.6 26.4 %collective-permute-start = (bf16[480,2048]{1,0:T(8,128)(2,1)}, bf16[480,2048]{1,0:T(8,128)(2,1)S(1)}, u32[]{:S(2)}, u32[]{:S(2)}) collective-permute-start(bf16[480,2048]{1,0:T(8,128)(2,1)} %get-tuple-element.334), channel_id=1, source_target_pairs={{0,1},{1,2},{2,3},{3,4},{4,5},{5,6},{6,7},{7,8},{8,9},{9,10},{10,1... | collective-permute-start | bytes 5898248 | tf_op jit(solution)/shard_map/while/body/eval_jaxpr/ppermute | solution.py:11
  401.2 3.7 copy-start.6
  404.9 2.8 copy-start.3
  410.1 1.9 copy-start.4
  412.0 26.4 %collective-permute-start = (bf16[480,2048]{1,0:T(8,128)(2,1)}, bf16[480,2048]{1,0:T(8,128)(2,1)S(1)}, u32[]{:S(2)}, u32[]{:S(2)}) collective-permute-start(bf16[480,2048]{1,0:T(8,128)(2,1)} %get-tuple-element.334), channel_id=1, source_target_pairs={{0,1},{1,2},{2,3},{3,4},{4,5},{5,6},{6,7},{7,8},{8,9},{9,10},{10,1... | collective-permute-start | bytes 5898248 | tf_op jit(solution)/shard_map/while/body/eval_jaxpr/ppermute | solution.py:11
  445.6 3.7 copy-start.6
  449.2 2.8 copy-start.3
  454.5 1.9 copy-start.4
  456.4 26.4 %collective-permute-start = (bf16[480,2048]{1,0:T(8,128)(2,1)}, bf16[480,2048]{1,0:T(8,128)(2,1)S(1)}, u32[]{:S(2)}, u32[]{:S(2)}) collective-permute-start(bf16[480,2048]{1,0:T(8,128)(2,1)} %get-tuple-element.334), channel_id=1, source_target_pairs={{0,1},{1,2},{2,3},{3,4},{4,5},{5,6},{6,7},{7,8},{8,9},{9,10},{10,1... | collective-permute-start | bytes 5898248 | tf_op jit(solution)/shard_map/while/body/eval_jaxpr/ppermute | solution.py:11
  490.0 3.7 copy-start.6
  493.6 2.8 copy-start.3
  498.9 1.9 copy-start.4
  500.8 26.4 %collective-permute-start = (bf16[480,2048]{1,0:T(8,128)(2,1)}, bf16[480,2048]{1,0:T(8,128)(2,1)S(1)}, u32[]{:S(2)}, u32[]{:S(2)}) collective-permute-start(bf16[480,2048]{1,0:T(8,128)(2,1)} %get-tuple-element.334), channel_id=1, source_target_pairs={{0,1},{1,2},{2,3},{3,4},{4,5},{5,6},{6,7},{7,8},{8,9},{9,10},{10,1... | collective-permute-start | bytes 5898248 | tf_op jit(solution)/shard_map/while/body/eval_jaxpr/ppermute | solution.py:11
  534.4 3.7 copy-start.6
  538.0 2.8 copy-start.3
  543.3 1.9 copy-start.4
  545.2 26.4 %collective-permute-start = (bf16[480,2048]{1,0:T(8,128)(2,1)}, bf16[480,2048]{1,0:T(8,128)(2,1)S(1)}, u32[]{:S(2)}, u32[]{:S(2)}) collective-permute-start(bf16[480,2048]{1,0:T(8,128)(2,1)} %get-tuple-element.334), channel_id=1, source_target_pairs={{0,1},{1,2},{2,3},{3,4},{4,5},{5,6},{6,7},{7,8},{8,9},{9,10},{10,1... | collective-permute-start | bytes 5898248 | tf_op jit(solution)/shard_map/while/body/eval_jaxpr/ppermute | solution.py:11
  578.7 3.7 copy-start.6
  582.4 2.8 copy-start.3
  587.7 1.9 copy-start.4
  589.6 26.4 %collective-permute-start = (bf16[480,2048]{1,0:T(8,128)(2,1)}, bf16[480,2048]{1,0:T(8,128)(2,1)S(1)}, u32[]{:S(2)}, u32[]{:S(2)}) collective-permute-start(bf16[480,2048]{1,0:T(8,128)(2,1)} %get-tuple-element.334), channel_id=1, source_target_pairs={{0,1},{1,2},{2,3},{3,4},{4,5},{5,6},{6,7},{7,8},{8,9},{9,10},{10,1... | collective-permute-start | bytes 5898248 | tf_op jit(solution)/shard_map/while/body/eval_jaxpr/ppermute | solution.py:11
  623.1 3.7 copy-start.6
  626.8 2.8 copy-start.3
  632.1 1.9 copy-start.4
  633.9 26.4 %collective-permute-start = (bf16[480,2048]{1,0:T(8,128)(2,1)}, bf16[480,2048]{1,0:T(8,128)(2,1)S(1)}, u32[]{:S(2)}, u32[]{:S(2)}) collective-permute-start(bf16[480,2048]{1,0:T(8,128)(2,1)} %get-tuple-element.334), channel_id=1, source_target_pairs={{0,1},{1,2},{2,3},{3,4},{4,5},{5,6},{6,7},{7,8},{8,9},{9,10},{10,1... | collective-permute-start | bytes 5898248 | tf_op jit(solution)/shard_map/while/body/eval_jaxpr/ppermute | solution.py:11
  667.5 3.7 copy-start.6
  671.2 2.8 copy-start.3
  676.5 1.9 copy-start.4
  678.3 26.4 %collective-permute-start = (bf16[480,2048]{1,0:T(8,128)(2,1)}, bf16[480,2048]{1,0:T(8,128)(2,1)S(1)}, u32[]{:S(2)}, u32[]{:S(2)}) collective-permute-start(bf16[480,2048]{1,0:T(8,128)(2,1)} %get-tuple-element.334), channel_id=1, source_target_pairs={{0,1},{1,2},{2,3},{3,4},{4,5},{5,6},{6,7},{7,8},{8,9},{9,10},{10,1... | collective-permute-start | bytes 5898248 | tf_op jit(solution)/shard_map/while/body/eval_jaxpr/ppermute | solution.py:11
  711.9 3.7 copy-start.6
  715.6 2.8 copy-start.3
  720.8 1.9 copy-start.4
  (16 other events, 20.5 us)
where the time goes:
time: 730 us; the launch traced here: 726 us
  waiting for transfers between devices  404 us (55%)
  local copies, waits for them, and re-layouts  198 us (27%)
  matrix products  102 us (14%)
  other arithmetic  13.7 us (2%)
  starting transfers between devices  8.23 us (1%)
    ppermute x15, waiting for transfers between devices, shifted(): lax.ppermute(x, axis, [(i, (i + by) % length) for i in range(length)])  381 us
    while x135, local copies, waits for them, and re-layouts  90 us
    dot_general x16, matrix products, contribute(): lax.dot_general(resident, passing, (((1,), (1,)), ((), ())), preferred_el...  60.2 us
    convert_element_type x32, local copies, waits for them, and re-layouts, contribute(): combined = combined.astype(jnp.bfloat16)  55.6 us
    dot_general x16, matrix products, contribute(): jnp.dot(combined, passing, preferred_element_type=jnp.float32)  41.4 us
    reshape x16, local copies, waits for them, and re-layouts, contribute(): amp_four = amplitude.reshape(CAP, vir_width, CAP, vir_width)  29.5 us
    all_to_all x1, waiting for transfers between devices, on_device(): lax.all_to_all(outgoing, 'occ', split_axis=0, concat_axis=3, tiled=True)  23.2 us
  transfers between devices with their start and end apart: 16, of which 16 were waited for; matrix products, arithmetic and copies ran while one was open for 2% of the time, Pallas kernels for 0%

commit v1 on v0

v1 whole, which is shorter than its diff:
```python
import functools

import jax
import jax.numpy as jnp
from jax import lax
from jax.experimental import pallas as pl
from jax.experimental.pallas import tpu as pltpu
from jax.sharding import PartitionSpec as P

CAP = 6
N_OCC = 8
N_VIRT = 16
ROWS = 16
MESH = pl.DeviceIdType.MESH

LEFT, RIGHT, ACROSS, FAR_A, FAR_B, LEFT_X, RIGHT_X, FAR_X = range(8)
N_LINK = 8
B_OWN, B_LEFT, B_RIGHT, B_ACROSS, B_FAR, B_LEFT_X, B_RIGHT_X, B_FAR_X = range(8)
N_SIB = 8


def kernel(
    phases, outgoing, row_gap, col_gap, out, whole, own, coul, amp, acc,
    a2a_send, a2a_recv, link_send, link_recv, sib_send, sib_recv, local_sem,
):
    occ = lax.axis_index("occ")
    me = lax.axis_index("virt")
    x, y, core = me // 4, (me // 2) % 2, me % 2
    slab = outgoing.shape[3]
    width = N_VIRT * ROWS

    def block(dx, flip):
        return ((x + dx) % 4) * 4 + (y + flip) % 2 * 2 + core

    right, left, across = block(1, 0), block(3, 0), block(0, 1)
    sibling = me + 1 - 2 * core

    barrier = pltpu.get_barrier_semaphore()
    for d in range(1, N_OCC):
        pl.semaphore_signal(
            barrier, inc=1, device_id={"occ": (occ + d) % N_OCC}, device_id_type=MESH
        )
    for peer in (right, left, across, sibling):
        pl.semaphore_signal(barrier, inc=1, device_id={"virt": peer}, device_id_type=MESH)
    pl.semaphore_wait(barrier, N_OCC + 3)

    my_slab = pl.ds(pl.multiple_of(occ * slab, slab), slab)

    def exchange(q, d):
        target = (occ + d) % N_OCC
        rows = pl.ds(pl.multiple_of(q * ROWS, ROWS), ROWS)
        return pltpu.make_async_remote_copy(
            src_ref=outgoing.at[target, :, rows, :],
            dst_ref=whole.at[q, :, me, :, my_slab],
            send_sem=a2a_send.at[q, d - 1],
            recv_sem=a2a_recv.at[q, d - 1],
            device_id={"occ": target},
            device_id_type=MESH,
        )

    def keep(q):
        rows = pl.ds(pl.multiple_of(q * ROWS, ROWS), ROWS)
        return pltpu.make_async_copy(
            outgoing.at[occ, :, rows, :], whole.at[q, :, me, :, my_slab], local_sem.at[q]
        )

    def link(q, source, kind, peer, first=0, count=CAP):
        part = whole.at[q, pl.ds(first, count), source]
        return pltpu.make_async_remote_copy(
            src_ref=part, dst_ref=part,
            send_sem=link_send.at[q, kind], recv_sem=link_recv.at[q, kind],
            device_id={"virt": peer}, device_id_type=MESH,
        )

    half = CAP // 2
    sends = {
        LEFT: (lambda q: link(q, me, LEFT, right)),
        RIGHT: (lambda q: link(q, me, RIGHT, left)),
        ACROSS: (lambda q: link(q, me, ACROSS, across)),
        FAR_A: (lambda q: link(q, left, FAR_A, right, 0, half)),
        FAR_B: (lambda q: link(q, right, FAR_B, left, half, CAP - half)),
        LEFT_X: (lambda q: link(q, across, LEFT_X, right)),
        RIGHT_X: (lambda q: link(q, across, RIGHT_X, left)),
        FAR_X: (lambda q: link(q, block(2, 0), FAR_X, across)),
    }
    held = {
        B_OWN: me, B_LEFT: left, B_RIGHT: right, B_ACROSS: across, B_FAR: block(2, 0),
        B_LEFT_X: block(3, 1), B_RIGHT_X: block(1, 1), B_FAR_X: block(2, 1),
    }

    def share(q, kind):
        part = whole.at[q, :, held[kind]]
        return pltpu.make_async_remote_copy(
            src_ref=part, dst_ref=part,
            send_sem=sib_send.at[q, kind], recv_sem=sib_recv.at[q, kind],
            device_id={"virt": sibling}, device_id_type=MESH,
        )

    def launch(q, _):
        for d in range(1, N_OCC):
            exchange(q, d).start()
        keep(q).start()
        return 0

    lax.fori_loop(0, phases, launch, 0)
    acc[...] = jnp.zeros_like(acc)

    def begin(q):
        for d in range(1, N_OCC):
            exchange(q, d).wait_recv()
        keep(q).wait()
        for kind in (LEFT, RIGHT, ACROSS):
            sends[kind](q).start()
        share(q, B_OWN).start()
        own[pl.ds(pl.multiple_of(q * CAP * ROWS, ROWS), CAP * ROWS), :] = whole[q, :, me].reshape(
            CAP * ROWS, own.shape[1]
        )

    def forward(q):
        sends[LEFT](q).wait_recv()
        sends[FAR_A](q).start()
        share(q, B_LEFT).start()
        sends[RIGHT](q).wait_recv()
        sends[FAR_B](q).start()
        share(q, B_RIGHT).start()
        sends[ACROSS](q).wait_recv()
        sends[LEFT_X](q).start()
        sends[RIGHT_X](q).start()
        share(q, B_ACROSS).start()

    def relay(q):
        sends[FAR_A](q).wait_recv()
        sends[FAR_B](q).wait_recv()
        sends[FAR_X](q).start()
        share(q, B_FAR).start()
        sends[LEFT_X](q).wait_recv()
        share(q, B_LEFT_X).start()
        sends[RIGHT_X](q).wait_recv()
        share(q, B_RIGHT_X).start()

    def last(q):
        sends[FAR_X](q).wait_recv()
        share(q, B_FAR_X).start()

    def compute(q):
        for kind in range(N_SIB):
            share(q, kind).wait_recv()

        def coulomb(j, _):
            coul[j] = lax.dot_general(
                own[...], whole[q, j].reshape(width, own.shape[1]),
                (((1,), (1,)), ((), ())), preferred_element_type=jnp.float32,
            )
            return 0

        lax.fori_loop(0, CAP, coulomb, 0)

        def combine(p, _):
            for i in range(CAP):
                at_i = pl.ds(pl.multiple_of(p * CAP * ROWS + i * ROWS, ROWS), ROWS)
                gap_i = row_gap[at_i, :]
                for j in range(i, CAP):
                    at_j = pl.ds(pl.multiple_of(p * CAP * ROWS + j * ROWS, ROWS), ROWS)
                    inverse = 1.0 / (gap_i + col_gap[q, pl.ds(j, 1), :])
                    direct = coul[j, at_i, :]
                    swapped = coul[i, at_j, :]
                    amp[at_i, j * width:(j + 1) * width] = (
                        (2.0 * direct - swapped) * inverse
                    ).astype(jnp.bfloat16)
                    if i != j:
                        amp[at_j, i * width:(i + 1) * width] = (
                            (2.0 * swapped - direct) * inverse
                        ).astype(jnp.bfloat16)
            return 0

        lax.fori_loop(0, phases, combine, 0)

        def density(n, _):
            at = pl.ds(pl.multiple_of(n * 256, 256), 256)
            acc[:, at] += jnp.dot(
                amp[...], whole[q, :, :, :, at].reshape(CAP * width, 256),
                preferred_element_type=jnp.float32,
            )
            return 0

        lax.fori_loop(0, acc.shape[1] // 256, density, 0)

    def step(t, _):
        pl.when(t < phases)(lambda: begin(t))
        pl.when((t >= 1) & (t < phases + 1))(lambda: forward(t - 1))
        pl.when((t >= 2) & (t < phases + 2))(lambda: relay(t - 2))
        pl.when((t >= 3) & (t < phases + 3))(lambda: last(t - 3))
        pl.when(t >= 4)(lambda: compute(t - 4))
        return 0

    lax.fori_loop(0, phases + 4, step, 0)

    for q in range(phases):
        for i in range(CAP):
            row = (q * CAP + i) * ROWS
            out[i, q * ROWS:(q + 1) * ROWS, :] = acc[row:row + ROWS, :].astype(out.dtype)

    def drain(q, _):
        for d in range(1, N_OCC):
            exchange(q, d).wait_send()
        for kind in range(N_LINK):
            sends[kind](q).wait_send()
        for kind in range(N_SIB):
            share(q, kind).wait_send()
        return 0

    lax.fori_loop(0, phases, drain, 0)


def on_device(basis_integrals, group_sizes, orbital_order, eps_occ, eps_vir):
    me_occ = lax.axis_index("occ")
    me_virt = lax.axis_index("virt")
    window, vir_width, slab = basis_integrals.shape
    phases = vir_width // ROWS
    naux = slab * N_OCC
    slot_index = jnp.arange(CAP, dtype=jnp.int32)
    offsets = jnp.cumsum(group_sizes) - group_sizes
    occupied = slot_index[None, :] < group_sizes[:, None]
    position = jnp.clip(offsets[:, None] + slot_index[None, :], 0, window - 1)
    orbital = jnp.where(occupied, orbital_order[position], 0)
    slot_mask = jnp.where(occupied, 1.0, 0.0).astype(jnp.bfloat16)
    outgoing = basis_integrals[orbital] * slot_mask[:, :, None, None]
    my_orbitals = lax.dynamic_index_in_dim(orbital, me_occ, 0, keepdims=False)
    my_alive = lax.dynamic_index_in_dim(occupied, me_occ, 0, keepdims=False)
    occ_energy = jnp.where(my_alive, eps_occ[my_orbitals], jnp.float32(0.0))
    by_phase = eps_vir.reshape(N_VIRT, phases, ROWS).transpose(1, 0, 2)
    own_energy = lax.dynamic_index_in_dim(by_phase, me_virt, 1, keepdims=False)
    row_gap = (occ_energy[None, :, None] - own_energy[:, None, :]).reshape(-1, 1)
    col_gap = occ_energy[None, :, None] - by_phase.reshape(phases, 1, N_VIRT * ROWS)
    rows, width = phases * CAP * ROWS, N_VIRT * ROWS
    dma = pltpu.SemaphoreType.DMA
    density = pl.pallas_call(
        functools.partial(kernel, phases),
        out_shape=jax.ShapeDtypeStruct((CAP, vir_width, naux), jnp.bfloat16),
        in_specs=[
            pl.BlockSpec(memory_space=pl.ANY),
            pl.BlockSpec(memory_space=pltpu.VMEM),
            pl.BlockSpec(memory_space=pltpu.VMEM),
        ],
        out_specs=pl.BlockSpec(memory_space=pltpu.VMEM),
        scratch_shapes=[
            pltpu.VMEM((phases, CAP, N_VIRT, ROWS, naux), jnp.bfloat16),
            pltpu.VMEM((rows, naux), jnp.bfloat16),
            pltpu.VMEM((CAP, rows, width), jnp.float32),
            pltpu.VMEM((rows, CAP * width), jnp.bfloat16),
            pltpu.VMEM((rows, naux), jnp.float32),
            dma((phases, N_OCC - 1)),
            dma((phases, N_OCC - 1)),
            dma((phases, N_LINK)),
            dma((phases, N_LINK)),
            dma((phases, N_SIB)),
            dma((phases, N_SIB)),
            dma((phases,)),
        ],
        compiler_params=pltpu.CompilerParams(
            collective_id=0, has_side_effects=True, vmem_limit_bytes=60 * 1024 * 1024
        ),
    )(outgoing, row_gap, col_gap)
    return density[None]


def solution(mesh):
    return jax.shard_map(
        on_device,
        mesh=mesh,
        in_specs=(P(None, "virt", "occ"), P(), P(), P(), P()),
        out_specs=P("occ", None, "virt", None),
        check_vma=False,
    )
```

time: 730 us -> 169 us (0.23)
  waiting for transfers between devices: 404 us -> 0 us
  local copies, waits for them, and re-layouts: 198 us -> 6.53 us
  Pallas kernels: 0 us -> 158 us
  matrix products: 102 us -> 0 us
  other arithmetic: 13.7 us -> 4.24 us
  starting transfers between devices: 8.23 us -> 0 us
    ppermute x15 -> x0, waiting for transfers between devices: 381 us -> none  [shifted(): lax.ppermute(x, axis, [(i, (i + by) % length) for i in range(length)])]
    pallas_call x0 -> x1, Pallas kernels: none -> 158 us  [on_device(): pl.pallas_call(functools.partial(kernel, phases), out_shape=jax.ShapeDtyp...]
    dot_general x32 -> x0, matrix products: 102 us -> none  [the longest x16 60.2 us: contribute(): lax.dot_general(resident, passing, (((1,), (1,)), ((), ())), preferred_el...]
    while x135 -> x0, local copies, waits for them, and re-layouts: 90 us -> none
    convert_element_type x32 -> x0, local copies, waits for them, and re-layouts: 55.6 us -> none  [contribute(): combined = combined.astype(jnp.bfloat16)]
    reshape x16 -> x1, local copies, waits for them, and re-layouts: 29.5 us -> 0.08 us  [on_device(): by_phase = eps_vir.reshape(N_VIRT, phases, ROWS).transpose(1, 0, 2)]
    all_to_all x1 -> x0, waiting for transfers between devices: 23.2 us -> none  [on_device(): lax.all_to_all(outgoing, 'occ', split_axis=0, concat_axis=3, tiled=True)]
    dynamic_slice x16 -> x0, local copies, waits for them, and re-layouts: 12.3 us -> none  [the longest x15 11.5 us: contribute(): lax.dynamic_slice_in_dim(eps_vir, anchor * vir_width, vir_width)]
  transfers between devices with their start and end apart: 16 -> 0, of which waited for: 16 -> 0; matrix products, arithmetic and copies ran while one was open for 2% -> 0% of each run, Pallas kernels for 0% -> 0%
where the time goes in v1:
time: 169 us
  Pallas kernels  158 us (93%)
  local copies, waits for them, and re-layouts  6.53 us (4%)
  other arithmetic  4.24 us (3%)
    pallas_call x1, Pallas kernels, on_device(): pl.pallas_call(functools.partial(kernel, phases), out_shape=jax.ShapeDtyp...  158 us

profile of v1, /device:TPU:0, one launch (start us, length us, event | category | flops | bytes accessed | tf_op | source)
XLA Modules:
  0.0 168.6 jit_solution(8657341970594496865)
XLA Ops:
  0.0 0.0 copy-start
  0.0 0.0 copy-start.1
  0.0 0.9 reduce-window.9
  1.0 0.7 bitcast_subtract_fusion
  1.6 0.1 compare_select_fusion.1
  1.7 0.1 reshape.207
  1.8 0.0 copy-done.1
  1.8 0.0 copy-start.4
  1.8 0.8 gather_fusion
  2.6 0.1 gather.12
  2.7 0.0 copy-done.4
  2.7 0.1 compare_select_fusion
  2.7 0.1 reshape.215
  2.8 0.0 copy-done
  2.8 0.7 gather_fusion.1
  3.5 0.1 select_convert_fusion
  3.6 0.0 copy-start.3
  3.6 0.0 copy-start.2
  3.6 1.5 broadcast_multiply_fusion.outgoing
  5.1 0.0 copy-done.3
  5.1 0.1 reshape.204
  5.2 0.1 reshape.206
  5.3 0.1 fusion
  5.4 0.0 copy-done.2
  5.4 0.6 gather_fusion.2
  6.0 0.1 iota_compare_fusion
  6.1 0.1 broadcast_subtract_fusion.1
  6.2 0.9 sub.53.row_gap
  7.1 0.1 sub.50
  7.1 0.7 broadcast_subtract_fusion.col_gap
  7.8 157.7 %shard_map.55 = bf16[6,80,2048]{2,1,0:T(8,128)(2,1)} custom-call(bf16[8,6,80,256]{3,2,1,0:T(8,128)(2,1)} %broadcast_multiply_fusion.outgoing, f32[480,1]{1,0:T(8,128)} %sub.53.row_gap, f32[5,6,256]{2,1,0:T(8,128)} %broadcast_subtract_fusion.col_gap), custom_call_target="tpu_custom_call" | custom-call | tf_op jit(solution)/shard_map/pallas_call | solution.py:237
  165.6 3.0 %copy.9 = bf16[1,6,80,2048]{3,2,1,0:T(8,128)(2,1)} copy(bf16[1,6,80,2048]{3,2,1,0:T(8,128)(2,1)} %bitcast.23) | data formatting | bytes 3932160
  (7 shorter events, 0.1 us)
Async XLA Ops:
  0.0 2.8 %copy-start = (bf16[32,80,256]{2,1,0:T(8,128)(2,1)S(1)}, bf16[32,80,256]{2,1,0:T(8,128)(2,1)}, u32[]{:S(2)}) copy-start(bf16[32,80,256]{2,1,0:T(8,128)(2,1)} %param.5) | copy-start | bytes 3932164
  0.0 1.8 %copy-start.1 = (s32[32]{0:T(128)S(1)}, s32[32]{0:T(128)}, u32[]{:S(2)}) copy-start(s32[32]{0:T(128)} %param.7) | copy-start | bytes 388
  1.8 0.9 copy-start.4
  3.6 1.5 copy-start.3
  3.6 1.8 %copy-start.2 = (f32[32]{0:T(128)S(1)}, f32[32]{0:T(128)}, u32[]{:S(2)}) copy-start(f32[32]{0:T(128)} %param.8) | copy-start | bytes 388

commit v2 on v1

v2 whole, which is shorter than its diff:
```python
import functools

import jax
import jax.numpy as jnp
from jax import lax
from jax.experimental import pallas as pl
from jax.experimental.pallas import tpu as pltpu
from jax.sharding import PartitionSpec as P

CAP = 6
N_OCC = 8
N_VIRT = 16
ROWS = 16
HALF = 8 * ROWS
MESH = pl.DeviceIdType.MESH

LEFT, RIGHT, ACROSS, FAR_A, FAR_B, LEFT_X, RIGHT_X, FAR_X = range(8)
N_LINK = 8
B_OWN, B_LEFT, B_RIGHT, B_ACROSS, B_FAR, B_LEFT_X, B_RIGHT_X, B_FAR_X = range(8)
N_SIB = 8


def kernel(
    phases, sizes, order, eps_occ, basis, eps_vir, out,
    whole, own, coul, amp, acc, outgoing, row_gap, col_gap,
    a2a_send, a2a_recv, link_send, link_recv, sib_send, sib_recv, local_sem,
):
    occ = lax.axis_index("occ")
    me = lax.axis_index("virt")
    x, y, core = me // 4, (me // 2) % 2, me % 2
    slab = outgoing.shape[4]
    rows_per = CAP * ROWS

    def device(dx, flip):
        return (x + dx) % 4 * 4 + (y + flip) % 2 * 2 + core

    def place(dx, flip):
        return (y + flip) % 2, (x + dx) % 4 * 2 + core

    right, left, across = device(1, 0), device(3, 0), device(0, 1)
    sibling = me + 1 - 2 * core
    column_of = x * 2 + core
    mine = place(0, 0)

    barrier = pltpu.get_barrier_semaphore()
    for d in range(1, N_OCC):
        pl.semaphore_signal(
            barrier, inc=1, device_id={"occ": (occ + d) % N_OCC}, device_id_type=MESH
        )
    for peer in (right, left, across, sibling):
        pl.semaphore_signal(barrier, inc=1, device_id={"virt": peer}, device_id_type=MESH)

    offset = jnp.int32(0)
    energy = [jnp.float32(0.0)] * CAP
    for g in range(N_OCC):
        size = sizes[g]
        for s in range(CAP):
            orbital = order[jnp.minimum(offset + s, order.shape[0] - 1)]
            alive = jnp.where(s < size, 1.0, 0.0)
            block = basis[orbital] * jnp.full((phases * ROWS, slab), alive).astype(jnp.bfloat16)
            for q in range(phases):
                outgoing[q, g, s] = block[q * ROWS:(q + 1) * ROWS]
            energy[s] = jnp.where(occ == g, alive * eps_occ[orbital], energy[s])
        offset = offset + size
    pl.semaphore_wait(barrier, N_OCC + 3)

    my_slab = pl.ds(pl.multiple_of(occ * slab, slab), slab)

    def exchange(q, d):
        target = (occ + d) % N_OCC
        return pltpu.make_async_remote_copy(
            src_ref=outgoing.at[q, target],
            dst_ref=whole.at[q, y, :, column_of, :, my_slab],
            send_sem=a2a_send.at[q, d - 1],
            recv_sem=a2a_recv.at[q, d - 1],
            device_id={"occ": target},
            device_id_type=MESH,
        )

    def keep(q):
        return pltpu.make_async_copy(
            outgoing.at[q, occ], whole.at[q, y, :, column_of, :, my_slab], local_sem.at[q]
        )

    def link(q, source, kind, peer, first=0, count=CAP):
        part = whole.at[q, source[0], pl.ds(first, count), source[1]]
        return pltpu.make_async_remote_copy(
            src_ref=part, dst_ref=part,
            send_sem=link_send.at[q, kind], recv_sem=link_recv.at[q, kind],
            device_id={"virt": peer}, device_id_type=MESH,
        )

    half = CAP // 2
    sends = {
        LEFT: (lambda q: link(q, mine, LEFT, right)),
        RIGHT: (lambda q: link(q, mine, RIGHT, left)),
        ACROSS: (lambda q: link(q, mine, ACROSS, across)),
        FAR_A: (lambda q: link(q, place(3, 0), FAR_A, right, 0, half)),
        FAR_B: (lambda q: link(q, place(1, 0), FAR_B, left, half, CAP - half)),
        LEFT_X: (lambda q: link(q, place(0, 1), LEFT_X, right)),
        RIGHT_X: (lambda q: link(q, place(0, 1), RIGHT_X, left)),
        FAR_X: (lambda q: link(q, place(2, 0), FAR_X, across)),
    }
    held = {
        B_OWN: mine, B_LEFT: place(3, 0), B_RIGHT: place(1, 0), B_ACROSS: place(0, 1),
        B_FAR: place(2, 0), B_LEFT_X: place(3, 1), B_RIGHT_X: place(1, 1), B_FAR_X: place(2, 1),
    }

    def share(q, kind):
        part = whole.at[q, held[kind][0], :, held[kind][1]]
        return pltpu.make_async_remote_copy(
            src_ref=part, dst_ref=part,
            send_sem=sib_send.at[q, kind], recv_sem=sib_recv.at[q, kind],
            device_id={"virt": sibling}, device_id_type=MESH,
        )

    def launch(q, _):
        for d in range(1, N_OCC):
            exchange(q, d).start()
        keep(q).start()
        return 0

    lax.fori_loop(0, phases, launch, 0)

    lane = lax.broadcasted_iota(jnp.int32, (ROWS, HALF), 1)
    sub = lax.broadcasted_iota(jnp.int32, (ROWS, HALF), 0)
    first_lane = column_of * ROWS
    for q in range(phases):
        spread = jnp.broadcast_to(eps_vir[pl.ds(q * 2 + y, 1), :], (ROWS, HALF))
        column = jnp.sum(
            jnp.where(lane == sub + first_lane, spread, 0.0), axis=1, keepdims=True
        )
        for i in range(CAP):
            at = (q * CAP + i) * ROWS
            row_gap[at:at + ROWS, :] = energy[i] - jnp.broadcast_to(column, (ROWS, HALF))
            for h in range(2):
                col_gap[q, h, i:i + 1, :] = energy[i] - eps_vir[q * 2 + h:q * 2 + h + 1, :]
    acc[...] = jnp.zeros_like(acc)

    def begin(q):
        for d in range(1, N_OCC):
            exchange(q, d).wait_recv()
        keep(q).wait()
        for kind in (LEFT, RIGHT, ACROSS):
            sends[kind](q).start()
        share(q, B_OWN).start()
        own[pl.ds(pl.multiple_of(q * rows_per, rows_per), rows_per), :] = whole[q, y, :, column_of].reshape(
            rows_per, own.shape[1]
        )

    def forward(q):
        sends[LEFT](q).wait_recv()
        sends[FAR_A](q).start()
        share(q, B_LEFT).start()
        sends[RIGHT](q).wait_recv()
        sends[FAR_B](q).start()
        share(q, B_RIGHT).start()
        sends[ACROSS](q).wait_recv()
        sends[LEFT_X](q).start()
        sends[RIGHT_X](q).start()
        share(q, B_ACROSS).start()

    def relay_far(q):
        sends[FAR_A](q).wait_recv()
        sends[FAR_B](q).wait_recv()
        sends[FAR_X](q).start()
        share(q, B_FAR).start()

    def relay_rest(q):
        sends[LEFT_X](q).wait_recv()
        share(q, B_LEFT_X).start()
        sends[RIGHT_X](q).wait_recv()
        share(q, B_RIGHT_X).start()
        sends[FAR_X](q).wait_recv()
        share(q, B_FAR_X).start()

    def compute(q, h, kinds):
        for kind in kinds:
            share(q, kind).wait_recv()

        def coulomb(j, _):
            coul[j] = lax.dot_general(
                own[...], whole[q, h, pl.ds(j * 2, 2)].reshape(2 * HALF, own.shape[1]),
                (((1,), (1,)), ((), ())), preferred_element_type=jnp.float32,
            )
            return 0

        lax.fori_loop(0, CAP // 2, coulomb, 0)

        def combine(p, _):
            def lanes(j):
                return slice(j % 2 * HALF, (j % 2 + 1) * HALF)

            for i in range(CAP):
                at_i = pl.ds(pl.multiple_of(p * rows_per + i * ROWS, ROWS), ROWS)
                gap_i = row_gap[at_i, :]
                for j in range(i, CAP):
                    at_j = pl.ds(pl.multiple_of(p * rows_per + j * ROWS, ROWS), ROWS)
                    inverse = 1.0 / (gap_i + col_gap[q, h, pl.ds(j, 1), :])
                    direct = coul[j // 2, at_i, lanes(j)]
                    swapped = coul[i // 2, at_j, lanes(i)]
                    amp[at_i, j * HALF:(j + 1) * HALF] = (
                        (2.0 * direct - swapped) * inverse
                    ).astype(jnp.bfloat16)
                    if i != j:
                        amp[at_j, i * HALF:(i + 1) * HALF] = (
                            (2.0 * swapped - direct) * inverse
                        ).astype(jnp.bfloat16)
            return 0

        lax.fori_loop(0, phases, combine, 0)

        def density(n, _):
            at = pl.ds(pl.multiple_of(n * 256, 256), 256)
            acc[:, at] += jnp.dot(
                amp[...], whole[q, h, :, :, :, at].reshape(CAP * HALF, 256),
                preferred_element_type=jnp.float32,
            )
            return 0

        lax.fori_loop(0, acc.shape[1] // 256, density, 0)

    def step(t, _):
        pl.when(2 * t < phases)(lambda: begin(2 * t))
        pl.when(2 * t + 1 < phases)(lambda: begin(2 * t + 1))
        pl.when((t >= 1) & (t < phases + 1))(lambda: forward(t - 1))
        pl.when((t >= 2) & (t < phases + 2))(lambda: relay_far(t - 2))
        pl.when(t >= 3)(
            lambda: compute(t - 3, 1 - y, (B_ACROSS, B_LEFT_X, B_RIGHT_X, B_FAR_X))
        )

        @pl.when((t >= 2) & (t < phases + 2))
        def _():
            compute(t - 2, y, (B_OWN, B_LEFT, B_RIGHT, B_FAR))
            relay_rest(t - 2)

        return 0

    lax.fori_loop(0, phases + 3, step, 0)

    for q in range(phases):
        for i in range(CAP):
            row = (q * CAP + i) * ROWS
            out[i, q * ROWS:(q + 1) * ROWS, :] = acc[row:row + ROWS, :].astype(out.dtype)

    def drain(q, _):
        for d in range(1, N_OCC):
            exchange(q, d).wait_send()
        for kind in range(N_LINK):
            sends[kind](q).wait_send()
        for kind in range(N_SIB):
            share(q, kind).wait_send()
        return 0

    lax.fori_loop(0, phases, drain, 0)


def on_device(basis_integrals, group_sizes, orbital_order, eps_occ, eps_vir):
    window, vir_width, slab = basis_integrals.shape
    phases = vir_width // ROWS
    naux = slab * N_OCC
    rows = phases * CAP * ROWS
    eps_lanes = eps_vir.reshape(4, 2, 2, phases, ROWS).transpose(3, 1, 0, 2, 4)
    eps_lanes = eps_lanes.reshape(phases * 2, HALF)
    dma = pltpu.SemaphoreType.DMA
    vmem = pl.BlockSpec(memory_space=pltpu.VMEM)
    smem = pl.BlockSpec(memory_space=pltpu.SMEM)
    density = pl.pallas_call(
        functools.partial(kernel, phases),
        out_shape=jax.ShapeDtypeStruct((CAP, vir_width, naux), jnp.bfloat16),
        in_specs=[smem, smem, smem, vmem, vmem],
        out_specs=vmem,
        scratch_shapes=[
            pltpu.VMEM((phases, 2, CAP, N_VIRT // 2, ROWS, naux), jnp.bfloat16),
            pltpu.VMEM((rows, naux), jnp.bfloat16),
            pltpu.VMEM((CAP // 2, rows, 2 * HALF), jnp.float32),
            pltpu.VMEM((rows, CAP * HALF), jnp.bfloat16),
            pltpu.VMEM((rows, naux), jnp.float32),
            pltpu.VMEM((phases, N_OCC, CAP, ROWS, slab), jnp.bfloat16),
            pltpu.VMEM((rows, HALF), jnp.float32),
            pltpu.VMEM((phases, 2, CAP, HALF), jnp.float32),
            dma((phases, N_OCC - 1)),
            dma((phases, N_OCC - 1)),
            dma((phases, N_LINK)),
            dma((phases, N_LINK)),
            dma((phases, N_SIB)),
            dma((phases, N_SIB)),
            dma((phases,)),
        ],
        compiler_params=pltpu.CompilerParams(
            collective_id=0, has_side_effects=True, vmem_limit_bytes=60 * 1024 * 1024
        ),
    )(group_sizes, orbital_order, eps_occ, basis_integrals, eps_lanes)
    return density[None]


def solution(mesh):
    return jax.shard_map(
        on_device,
        mesh=mesh,
        in_specs=(P(None, "virt", "occ"), P(), P(), P(), P()),
        out_specs=P("occ", None, "virt", None),
        check_vma=False,
    )
```

time: 169 us -> 151 us (0.89); the launches traced: 169 us -> 149 us
  Pallas kernels: 158 us -> 144 us
  other arithmetic: 4.24 us -> 0 us
  local copies, waits for them, and re-layouts: 6.53 us -> 4.55 us
    pallas_call x1, Pallas kernels: 158 us -> 144 us  [on_device(): pl.pallas_call(functools.partial(kernel, phases), out_shape=jax.ShapeDtyp...]
    gather x5 -> x0, local copies, waits for them, and re-layouts: 2.25 us -> none  [the longest x3 0.93 us: on_device(): orbital = jnp.where(occupied, orbital_order[position], 0)]
where the time goes in v2:
time: 151 us; the launch traced here: 149 us
  Pallas kernels  144 us (95%)
  local copies, waits for them, and re-layouts  4.55 us (3%)
    pallas_call x1, Pallas kernels, on_device(): pl.pallas_call(functools.partial(kernel, phases), out_shape=jax.ShapeDtyp...  144 us
    unnamed x1, local copies, waits for them, and re-layouts  3.04 us

profile of v2, /device:TPU:0, one launch (start us, length us, event | category | flops | bytes accessed | tf_op | source)
XLA Modules:
  0.0 148.7 jit_solution(10121645203767243212)
XLA Ops:
  0.0 0.8 reshape.6
  0.8 0.7 reshape.7.eps_vir
  1.5 144.1 %shard_map.55 = bf16[6,80,2048]{2,1,0:T(8,128)(2,1)} custom-call(s32[8]{0:T(128)} %sizes.1, s32[32]{0:T(128)} %order.1, f32[32]{0:T(128)} %eps_occ.1, bf16[32,80,256]{2,1,0:T(8,128)(2,1)} %basis.1, f32[10,128]{1,0:T(8,128)} %reshape.7.eps_vir), custom_call_target="tpu_custom_call" | custom-call | tf_op jit(solution)/shard_map/pallas_call | solution.py:268
  145.6 3.0 %copy.8 = bf16[1,6,80,2048]{3,2,1,0:T(8,128)(2,1)} copy(bf16[1,6,80,2048]{3,2,1,0:T(8,128)(2,1)} %bitcast.2) | data formatting | bytes 3932160
  (1 shorter events, 0.0 us)

commit v3 on v2

--- a/solution.py
+++ b/solution.py
@@ -137,24 +137,28 @@
                 col_gap[q, h, i:i + 1, :] = energy[i] - eps_vir[q * 2 + h:q * 2 + h + 1, :]
     acc[...] = jnp.zeros_like(acc)
 
-    def begin(q):
+    def gather_rows(q):
         for d in range(1, N_OCC):
             exchange(q, d).wait_recv()
         keep(q).wait()
+        own[pl.ds(pl.multiple_of(q * rows_per, rows_per), rows_per), :] = whole[
+            q, y, :, column_of
+        ].reshape(rows_per, own.shape[1])
+
+    def send_own(q):
         for kind in (LEFT, RIGHT, ACROSS):
             sends[kind](q).start()
         share(q, B_OWN).start()
-        own[pl.ds(pl.multiple_of(q * rows_per, rows_per), rows_per), :] = whole[q, y, :, column_of].reshape(
-            rows_per, own.shape[1]
-        )
-
-    def forward(q):
+
+    def forward_far(q):
         sends[LEFT](q).wait_recv()
         sends[FAR_A](q).start()
         share(q, B_LEFT).start()
         sends[RIGHT](q).wait_recv()
         sends[FAR_B](q).start()
         share(q, B_RIGHT).start()
+
+    def forward_across(q):
         sends[ACROSS](q).wait_recv()
         sends[LEFT_X](q).start()
         sends[RIGHT_X](q).start()
@@ -185,7 +189,7 @@
             )
             return 0
 
-        lax.fori_loop(0, CAP // 2, coulomb, 0)
+        lax.fori_loop(0, CAP // 2, coulomb, 0, unroll=True)
 
         def combine(p, _):
             def lanes(j):
@@ -211,32 +215,43 @@
         lax.fori_loop(0, phases, combine, 0)
 
         def density(n, _):
-            at = pl.ds(pl.multiple_of(n * 256, 256), 256)
+            at = pl.ds(pl.multiple_of(n * 512, 512), 512)
             acc[:, at] += jnp.dot(
-                amp[...], whole[q, h, :, :, :, at].reshape(CAP * HALF, 256),
+                amp[...], whole[q, h, :, :, :, at].reshape(CAP * HALF, 512),
                 preferred_element_type=jnp.float32,
             )
             return 0
 
-        lax.fori_loop(0, acc.shape[1] // 256, density, 0)
-
-    def step(t, _):
-        pl.when(2 * t < phases)(lambda: begin(2 * t))
-        pl.when(2 * t + 1 < phases)(lambda: begin(2 * t + 1))
-        pl.when((t >= 1) & (t < phases + 1))(lambda: forward(t - 1))
-        pl.when((t >= 2) & (t < phases + 2))(lambda: relay_far(t - 2))
-        pl.when(t >= 3)(
-            lambda: compute(t - 3, 1 - y, (B_ACROSS, B_LEFT_X, B_RIGHT_X, B_FAR_X))
-        )
-
-        @pl.when((t >= 2) & (t < phases + 2))
+        lax.fori_loop(0, acc.shape[1] // 512, density, 0, unroll=True)
+
+    final = phases - 1
+    for q in range(phases):
+        gather_rows(q)
+        if q < max(final, 1):
+            send_own(q)
+        if 1 <= q <= 2:
+            forward_far(q - 1)
+        if q == 2:
+            forward_across(0)
+
+    def step(k, _):
+        @pl.when(k < phases)
         def _():
-            compute(t - 2, y, (B_OWN, B_LEFT, B_RIGHT, B_FAR))
-            relay_rest(t - 2)
-
+            relay_far(k)
+            compute(k, y, (B_OWN, B_LEFT, B_RIGHT, B_FAR))
+
+        @pl.when(k >= 1)
+        def _():
+            relay_rest(k - 1)
+            compute(k - 1, 1 - y, (B_ACROSS, B_LEFT_X, B_RIGHT_X, B_FAR_X))
+
+        pl.when(k == 0)(lambda: send_own(final))
+        pl.when(k + 2 < phases)(lambda: forward_far(k + 2))
+        pl.when(k + 2 < phases)(lambda: forward_across(k + 1))
+        pl.when(k + 3 == phases)(lambda: forward_across(final))
         return 0
 
-    lax.fori_loop(0, phases + 3, step, 0)
+    lax.fori_loop(0, phases + 1, step, 0)
 
     for q in range(phases):
         for i in range(CAP):
@@ -288,7 +303,7 @@
             dma((phases,)),
         ],
         compiler_params=pltpu.CompilerParams(
-            collective_id=0, has_side_effects=True, vmem_limit_bytes=60 * 1024 * 1024
+            collective_id=0, has_side_effects=True, vmem_limit_bytes=47 * 1024 * 1024
         ),
     )(group_sizes, orbital_order, eps_occ, basis_integrals, eps_lanes)
     return density[None]

time: 151 us -> 143 us (0.947); the launches traced: 149 us -> 143 us
  Pallas kernels: 144 us -> 137 us
    pallas_call x1, Pallas kernels: 144 us -> 137 us  [on_device(): pl.pallas_call(functools.partial(kernel, phases), out_shape=jax.ShapeDtyp...]
    unnamed x1 -> x9, local copies, waits for them, and re-layouts: 3.04 us -> 4.56 us
where the time goes in v3:
time: 143 us
  Pallas kernels  137 us (96%)
  local copies, waits for them, and re-layouts  5.45 us (4%)
    pallas_call x1, Pallas kernels, on_device(): pl.pallas_call(functools.partial(kernel, phases), out_shape=jax.ShapeDtyp...  137 us
    unnamed x9, local copies, waits for them, and re-layouts  4.56 us

profile of v3, /device:TPU:0, one launch (start us, length us, event | category | flops | bytes accessed | tf_op | source)
XLA Modules:
  0.0 142.5 jit_solution(7177092130062027939)
XLA Ops:
  0.0 0.8 reshape.6
  0.8 0.1 reshape.7.eps_vir
  0.9 0.0 copy-start
  0.9 1.3 copy-done
  2.2 0.0 copy-start.1
  2.2 0.7 copy-done.1
  2.9 0.0 copy-start.2
  2.9 0.7 copy-done.2
  3.6 0.0 copy-start.3
  3.6 0.7 copy-done.3
  4.2 137.1 %shard_map.55 = bf16[6,80,2048]{2,1,0:T(8,128)(2,1)S(1)} custom-call(s32[8]{0:T(128)S(1)} %copy-done.1, s32[32]{0:T(128)S(1)} %copy-done.2, f32[32]{0:T(128)S(1)} %copy-done.3, bf16[32,80,256]{2,1,0:T(8,128)(2,1)S(1)} %copy-done, f32[10,128]{1,0:T(8,128)S(1)} %reshape.7.eps_vir), custom_call_target="tpu_custom_call" | custom-call | tf_op jit(solution)/shard_map/pallas_call | solution.py:283
  141.3 1.3 copy.8
  (1 shorter events, 0.0 us)
Async XLA Ops:
  0.9 1.3 copy-start
  2.2 0.7 copy-start.1
  2.9 0.7 copy-start.2
  3.6 0.7 copy-start.3

commit v4 on v3

--- a/solution.py
+++ b/solution.py
@@ -21,9 +21,9 @@
 
 
 def kernel(
-    phases, sizes, order, eps_occ, basis, eps_vir, out,
+    phases, sizes, order, eps_occ, basis_hbm, eps_vir, out,
     whole, own, coul, amp, acc, outgoing, row_gap, col_gap,
-    a2a_send, a2a_recv, link_send, link_recv, sib_send, sib_recv, local_sem,
+    eps_half, basis, basis_sem, a2a_send, a2a_recv, link_send, link_recv, sib_send, sib_recv, local_sem,
 ):
     occ = lax.axis_index("occ")
     me = lax.axis_index("virt")
@@ -42,6 +42,8 @@
     column_of = x * 2 + core
     mine = place(0, 0)
 
+    fetch = pltpu.make_async_copy(basis_hbm, basis, basis_sem)
+    fetch.start()
     barrier = pltpu.get_barrier_semaphore()
     for d in range(1, N_OCC):
         pl.semaphore_signal(
@@ -50,6 +52,7 @@
     for peer in (right, left, across, sibling):
         pl.semaphore_signal(barrier, inc=1, device_id={"virt": peer}, device_id_type=MESH)
 
+    fetch.wait()
     offset = jnp.int32(0)
     energy = [jnp.float32(0.0)] * CAP
     for g in range(N_OCC):
@@ -126,7 +129,17 @@
     sub = lax.broadcasted_iota(jnp.int32, (ROWS, HALF), 0)
     first_lane = column_of * ROWS
     for q in range(phases):
-        spread = jnp.broadcast_to(eps_vir[pl.ds(q * 2 + y, 1), :], (ROWS, HALF))
+        for h in range(2):
+            lanes = jnp.zeros((1, HALF), jnp.float32)
+            for k in range(8):
+                chunk = (k // 2 * 4 + h * 2 + k % 2) * phases + q
+                piece = eps_vir[chunk // 8:chunk // 8 + 1, :]
+                shift = (k - chunk % 8) % 8 * ROWS
+                piece = pltpu.roll(piece, shift, 1) if shift else piece
+                lanes = jnp.where(lane[:1] // ROWS == k, piece, lanes)
+            eps_half[q, h:h + 1, :] = lanes
+    for q in range(phases):
+        spread = jnp.broadcast_to(eps_half[q, pl.ds(y, 1), :], (ROWS, HALF))
         column = jnp.sum(
             jnp.where(lane == sub + first_lane, spread, 0.0), axis=1, keepdims=True
         )
@@ -134,7 +147,7 @@
             at = (q * CAP + i) * ROWS
             row_gap[at:at + ROWS, :] = energy[i] - jnp.broadcast_to(column, (ROWS, HALF))
             for h in range(2):
-                col_gap[q, h, i:i + 1, :] = energy[i] - eps_vir[q * 2 + h:q * 2 + h + 1, :]
+                col_gap[q, h, i:i + 1, :] = energy[i] - eps_half[q, h:h + 1, :]
     acc[...] = jnp.zeros_like(acc)
 
     def gather_rows(q):
@@ -240,15 +253,16 @@
             relay_far(k)
             compute(k, y, (B_OWN, B_LEFT, B_RIGHT, B_FAR))
 
+        pl.when(k == 0)(lambda: send_own(final))
+        pl.when(k + 2 < phases)(lambda: forward_far(k + 2))
+        pl.when(k + 2 < phases)(lambda: forward_across(k + 1))
+        pl.when(k + 3 == phases)(lambda: forward_across(final))
+
         @pl.when(k >= 1)
         def _():
             relay_rest(k - 1)
             compute(k - 1, 1 - y, (B_ACROSS, B_LEFT_X, B_RIGHT_X, B_FAR_X))
 
-        pl.when(k == 0)(lambda: send_own(final))
-        pl.when(k + 2 < phases)(lambda: forward_far(k + 2))
-        pl.when(k + 2 < phases)(lambda: forward_across(k + 1))
-        pl.when(k + 3 == phases)(lambda: forward_across(final))
         return 0
 
     lax.fori_loop(0, phases + 1, step, 0)
@@ -275,15 +289,13 @@
     phases = vir_width // ROWS
     naux = slab * N_OCC
     rows = phases * CAP * ROWS
-    eps_lanes = eps_vir.reshape(4, 2, 2, phases, ROWS).transpose(3, 1, 0, 2, 4)
-    eps_lanes = eps_lanes.reshape(phases * 2, HALF)
     dma = pltpu.SemaphoreType.DMA
     vmem = pl.BlockSpec(memory_space=pltpu.VMEM)
     smem = pl.BlockSpec(memory_space=pltpu.SMEM)
     density = pl.pallas_call(
         functools.partial(kernel, phases),
         out_shape=jax.ShapeDtypeStruct((CAP, vir_width, naux), jnp.bfloat16),
-        in_specs=[smem, smem, smem, vmem, vmem],
+        in_specs=[smem, smem, smem, pl.BlockSpec(memory_space=pltpu.HBM), vmem],
         out_specs=vmem,
         scratch_shapes=[
             pltpu.VMEM((phases, 2, CAP, N_VIRT // 2, ROWS, naux), jnp.bfloat16),
@@ -294,6 +306,9 @@
             pltpu.VMEM((phases, N_OCC, CAP, ROWS, slab), jnp.bfloat16),
             pltpu.VMEM((rows, HALF), jnp.float32),
             pltpu.VMEM((phases, 2, CAP, HALF), jnp.float32),
+            pltpu.VMEM((phases, 2, HALF), jnp.float32),
+            pltpu.VMEM((window, vir_width, slab), jnp.bfloat16),
+            dma,
             dma((phases, N_OCC - 1)),
             dma((phases, N_OCC - 1)),
             dma((phases, N_LINK)),
@@ -303,9 +318,9 @@
             dma((phases,)),
         ],
         compiler_params=pltpu.CompilerParams(
-            collective_id=0, has_side_effects=True, vmem_limit_bytes=47 * 1024 * 1024
+            collective_id=0, has_side_effects=True, vmem_limit_bytes=60 * 1024 * 1024
         ),
-    )(group_sizes, orbital_order, eps_occ, basis_integrals, eps_lanes)
+    )(group_sizes, orbital_order, eps_occ, basis_integrals, eps_vir.reshape(-1, HALF))
     return density[None]
 
 

time: 143 us -> 141 us (0.986)
  local copies, waits for them, and re-layouts: 5.45 us -> 3.04 us
    unnamed x9 -> x1, local copies, waits for them, and re-layouts: 4.56 us -> 3.04 us
where the time goes in v4:
time: 141 us; the launch traced here: 140 us
  Pallas kernels  136 us (96%)
  local copies, waits for them, and re-layouts  3.04 us (2%)
    pallas_call x1, Pallas kernels, on_device(): pl.pallas_call(functools.partial(kernel, phases), out_shape=jax.ShapeDtyp...  136 us
    unnamed x1, local copies, waits for them, and re-layouts  3.04 us

profile of v4, /device:TPU:0, one launch (start us, length us, event | category | flops | bytes accessed | tf_op | source)
XLA Modules:
  0.0 139.5 jit_solution(1879653727854713707)
XLA Ops:
  0.0 136.5 %shard_map.55 = bf16[6,80,2048]{2,1,0:T(8,128)(2,1)} custom-call(s32[8]{0:T(128)} %sizes.1, s32[32]{0:T(128)} %order.1, f32[32]{0:T(128)} %eps_occ.1, bf16[32,80,256]{2,1,0:T(8,128)(2,1)} %basis_hbm.1, f32[10,128]{1,0:T(8,128)} %bitcast.3), custom_call_target="tpu_custom_call" | custom-call | tf_op jit(solution)/shard_map/pallas_call | solution.py:295
  136.5 3.0 %copy.7 = bf16[1,6,80,2048]{3,2,1,0:T(8,128)(2,1)} copy(bf16[1,6,80,2048]{3,2,1,0:T(8,128)(2,1)} %bitcast.2) | data formatting | bytes 3932160

commit v5 on v4

--- a/solution.py
+++ b/solution.py
@@ -117,13 +117,13 @@
             device_id={"virt": sibling}, device_id_type=MESH,
         )
 
-    def launch(q, _):
+    def launch(q):
         for d in range(1, N_OCC):
             exchange(q, d).start()
         keep(q).start()
         return 0
 
-    lax.fori_loop(0, phases, launch, 0)
+    launch(0)
 
     lane = lax.broadcasted_iota(jnp.int32, (ROWS, HALF), 1)
     sub = lax.broadcasted_iota(jnp.int32, (ROWS, HALF), 0)
@@ -154,6 +154,8 @@
         for d in range(1, N_OCC):
             exchange(q, d).wait_recv()
         keep(q).wait()
+        if q + 1 < phases:
+            launch(q + 1)
         own[pl.ds(pl.multiple_of(q * rows_per, rows_per), rows_per), :] = whole[
             q, y, :, column_of
         ].reshape(rows_per, own.shape[1])

time: 141 us -> 138 us (0.979)
    pallas_call x1, Pallas kernels: 136 us -> 135 us  [on_device(): pl.pallas_call(functools.partial(kernel, phases), out_shape=jax.ShapeDtyp...]
where the time goes in v5:
time: 138 us
  Pallas kernels  135 us (98%)
  local copies, waits for them, and re-layouts  3.04 us (2%)
    pallas_call x1, Pallas kernels, on_device(): pl.pallas_call(functools.partial(kernel, phases), out_shape=jax.ShapeDtyp...  135 us
    unnamed x1, local copies, waits for them, and re-layouts  3.04 us

profile of v5, /device:TPU:0, one launch (start us, length us, event | category | flops | bytes accessed | tf_op | source)
XLA Modules:
  0.0 137.8 jit_solution(5943026525553062886)
XLA Ops:
  0.0 134.7 %shard_map.55 = bf16[6,80,2048]{2,1,0:T(8,128)(2,1)} custom-call(s32[8]{0:T(128)} %sizes.1, s32[32]{0:T(128)} %order.1, f32[32]{0:T(128)} %eps_occ.1, bf16[32,80,256]{2,1,0:T(8,128)(2,1)} %basis_hbm.1, f32[10,128]{1,0:T(8,128)} %bitcast.3), custom_call_target="tpu_custom_call" | custom-call | tf_op jit(solution)/shard_map/pallas_call | solution.py:297
  134.7 3.0 %copy.7 = bf16[1,6,80,2048]{3,2,1,0:T(8,128)(2,1)} copy(bf16[1,6,80,2048]{3,2,1,0:T(8,128)(2,1)} %bitcast.2) | data formatting | bytes 3932160
